TPU v7x, 32 devices: a whole 2x2x4 slice. The times are simulated.
32 devices in a mesh: row: 4 (over y, core), col: 8 (over z, x).
Axes of the slice: x: 2, y: 2, z: 4, core: 2. Of those that a mesh axis runs over, the one named last changes fastest.
Arguments:
- contribution: float32 [8, 4, 4, 8, 128, 128], P(None, 'row', None, 'col'), may hold values from -6 to 6
- parent_tiles: float32 [16, 4, 8, 8, 128, 128], P(None, 'row', None, 'col'), may hold values from -6 to 6
- row_basis: float32 [8, 4, 64, 128], P(None, 'row'), may hold values from -2.4 to 2.4
- pivot_basis: float32 [8, 4, 64, 2048], P(None, 'row', None, 'col'), may hold values from -0.125 to 0.125
- tile_ranks: int32 [32], replicated, may hold values from 16 to 64, as said below
- block_map: int32 [32], replicated, may hold values from 0 to 63, as said below
- panel_start: int32 [1], replicated, may hold values from 0 to 31
- pivot_inverse: float32 [512, 512], replicated
Outputs:
- updated_parent: float32 [16, 4, 8, 8, 128, 128], P(None, 'row', None, 'col')
Inputs may be any that keep to these rules, and one draw needn't show every extreme that they name: `tile_ranks`: multiples of 16; both 16 and 64 occur. `block_map`: child tile row u * 8 + l, for 0 <= l < 8, maps to parent tile row 2 * 8 * u + h_u + l with 0 <= h_u < 8; the 4 values h_u are distinct modulo 4.
All inputs are finite; a program needn't handle non-finite values.
Results may differ from a plain program's by a relative error of at most 0.0003.
Values sent between devices are 32-bit elements; how exact they have to be, the bound alone decides.
A program may use at most 128 MiB of HBM per device.

v0:
```python
import jax
import jax.numpy as jnp
from jax import lax
from jax.sharding import PartitionSpec as P

PANEL_T = 4


highest = lax.Precision.HIGHEST


def spread_2(x, axis, root):
    mine = lax.axis_index(axis) == root
    return lax.psum(jnp.where(mine, x, jnp.zeros_like(x)), axis)


def select_entries(lookup, wanted):
    matches = wanted[:, None] == jnp.arange(lookup.shape[0], dtype=jnp.int32)[None, :]
    return jnp.sum(jnp.where(matches, lookup[None, :], 0), axis=1)


def keep_ranks(factor, tile_index, rank_table):
    limits = select_entries(rank_table, tile_index)
    kept_cols = (jnp.arange(factor.shape[1], dtype=jnp.int32)[None, :] < limits[:, None]).astype(
        jnp.float32
    )
    return factor * kept_cols[:, :, None]


def every_other(stacked, groups, offset):
    shaped = stacked.reshape((groups, stacked.shape[0] // groups) + stacked.shape[1:])
    return lax.dynamic_index_in_dim(shaped, offset, axis=1, keepdims=False)


def per_device(
    contribution,
    parent_tiles,
    row_basis,
    pivot_basis,
    tile_ranks,
    block_map,
    panel_start,
    pivot_inverse,
):
    rows_grid = lax.axis_size("row")
    cols_grid = lax.axis_size("col")
    my_row = lax.axis_index("row")
    my_col = lax.axis_index("col")
    local_rows = contribution.shape[0]
    local_cols = contribution.shape[2]
    parent_rows = parent_tiles.shape[0]
    parent_cols = parent_tiles.shape[2]
    rank_max = row_basis.shape[2]
    per_block = cols_grid // rows_grid
    row_index = jnp.arange(local_rows, dtype=jnp.int32) * rows_grid + my_row
    col_index = jnp.arange(local_cols, dtype=jnp.int32) * cols_grid + my_col
    root_row = my_col % rows_grid
    offset = my_col // rows_grid
    own_basis = keep_ranks(row_basis[:, 0], row_index, tile_ranks)
    own_pivots = pivot_basis[:, 0]
    basis_picked = every_other(row_basis[:, 0], local_cols, offset)
    col_basis = spread_2(basis_picked, "row", root_row)
    all_pivots = lax.all_gather(pivot_basis, "row", axis=1, tiled=True)
    pivot_width = pivot_basis.shape[3]
    grouped = all_pivots.reshape(local_cols, cols_grid, rank_max, pivot_width)
    products = jnp.einsum(
        "trp,scup->cstru",
        own_pivots,
        grouped,
        precision=highest,
        preferred_element_type=jnp.float32,
    )
    weights = lax.psum_scatter(
        products.reshape(lax.axis_size("col") * local_cols, local_rows, rank_max * rank_max),
        "col",
        scatter_dimension=0,
        tiled=True,
    )
    weights = weights.reshape(local_cols, local_rows, rank_max, rank_max)
    col_basis = keep_ranks(col_basis, col_index, tile_ranks)
    half_product = jnp.einsum(
        "trx,stru->tsux", own_basis, weights, precision=highest, preferred_element_type=jnp.float32
    )
    update = jnp.einsum(
        "tsux,suy->tsxy",
        half_product,
        col_basis,
        precision=highest,
        preferred_element_type=jnp.float32,
    )
    lower_mask = (row_index[:, None] >= col_index[None, :])[:, :, None, None]
    payload = jnp.where(lower_mask, contribution[:, 0, :, 0] - update, jnp.float32(0.0))
    block_first = jnp.arange(local_cols, dtype=jnp.int32) * cols_grid
    shifts = select_entries(block_map, block_first) - 2 * block_first
    row_shift = jnp.repeat(shifts, per_block) % rows_grid
    positions = jnp.arange(local_rows, dtype=jnp.int32)
    grid_rows = jnp.arange(rows_grid, dtype=jnp.int32)
    block_rows = jnp.arange(per_block, dtype=jnp.int32)
    target = (my_row + row_shift) % rows_grid
    buckets = (target[None, None, :] == grid_rows[:, None, None]) & (
        positions[None, None, :] % per_block == block_rows[None, :, None]
    )
    packed = jnp.einsum(
        "rlt,tsxy->rlsxy",
        buckets.astype(jnp.float32),
        payload,
        precision=highest,
        preferred_element_type=jnp.float32,
    )
    arrived = lax.all_to_all(packed, "row", split_axis=0, concat_axis=0, tiled=True)
    source = (my_row - row_shift) % rows_grid
    chosen = (source[:, None, None] == grid_rows[None, :, None]) & (
        positions[:, None, None] % per_block == block_rows[None, None, :]
    )
    payload = jnp.einsum(
        "tpl,plsxy->tsxy",
        chosen.astype(jnp.float32),
        arrived,
        precision=highest,
        preferred_element_type=jnp.float32,
    )
    grid_cols = jnp.arange(cols_grid, dtype=jnp.int32)
    target = (my_col + shifts) % cols_grid
    buckets = (grid_cols[:, None] == target[None, :]).astype(jnp.float32)
    packed = jnp.einsum(
        "cs,tsxy->ctxy", buckets, payload, precision=highest, preferred_element_type=jnp.float32
    )
    arrived = lax.all_to_all(packed, "col", split_axis=0, concat_axis=0, tiled=True)
    source = (my_col - shifts) % cols_grid
    chosen = (source[:, None] == grid_cols[None, :]).astype(jnp.float32)
    payload = jnp.einsum(
        "sq,qtxy->tsxy", chosen, arrived, precision=highest, preferred_element_type=jnp.float32
    )
    row_source = (my_row - row_shift) % rows_grid
    target_rows = (
        select_entries(block_map, jnp.arange(local_rows, dtype=jnp.int32) * rows_grid + row_source)
        // rows_grid
    )
    col_source = (my_col - shifts) % cols_grid
    target_cols = (
        select_entries(block_map, jnp.arange(local_cols, dtype=jnp.int32) * cols_grid + col_source)
        // cols_grid
    )
    row_place = (jnp.arange(parent_rows, dtype=jnp.int32)[:, None] == target_rows[None, :]).astype(
        jnp.float32
    )
    col_place = (jnp.arange(parent_cols, dtype=jnp.int32)[:, None] == target_cols[None, :]).astype(
        jnp.float32
    )
    spread = jnp.einsum(
        "at,tsxy->asxy", row_place, payload, precision=highest, preferred_element_type=jnp.float32
    )
    spread = jnp.einsum(
        "bs,asxy->abxy", col_place, spread, precision=highest, preferred_element_type=jnp.float32
    )
    assembled = parent_tiles[:, 0, :, 0] + spread
    start_col = panel_start[0]
    panel_parts = []
    for panel_index in range(PANEL_T):
        column_id = start_col + panel_index
        column = lax.dynamic_index_in_dim(assembled, column_id // cols_grid, axis=1, keepdims=False)
        panel_parts.append(spread_2(column, "col", column_id % cols_grid))
    row_panel = jnp.concatenate(panel_parts, axis=2)
    col_panel = spread_2(every_other(row_panel, parent_cols, offset), "row", root_row)
    scaled = jnp.einsum(
        "axp,pq->axq",
        row_panel,
        pivot_inverse,
        precision=highest,
        preferred_element_type=jnp.float32,
    )
    trailing = jnp.einsum(
        "axq,byq->abxy", scaled, col_panel, precision=highest, preferred_element_type=jnp.float32
    )
    big_rows = jnp.arange(parent_rows, dtype=jnp.int32) * rows_grid + my_row
    big_cols = jnp.arange(parent_cols, dtype=jnp.int32) * cols_grid + my_col
    window = (big_rows[:, None] >= big_cols[None, :]) & (big_cols[None, :] >= start_col + PANEL_T)
    result = jnp.where(window[:, :, None, None], assembled - trailing, assembled)
    return result[:, None, :, None]


def solution(mesh):
    placed = (
        P(None, "row", None, "col", None, None),
        P(None, "row", None, "col", None, None),
        P(None, "row", None, None),
        P(None, "row", None, "col"),
        P(),
        P(),
        P(),
        P(),
    )
    return jax.shard_map(
        per_device,
        mesh=mesh,
        in_specs=placed,
        out_specs=P(None, "row", None, "col", None, None),
        check_vma=False,
    )
```

profile of v0, /device:TPU:21, one launch (start us, length us, event | category | flops | bytes accessed | tf_op | source)
XLA Modules:
  0.0 628.1 jit_solution(7358268247508881916)
XLA Ops:
  6.5 0.7 all-gather.2.cloned.1.call-update
  7.3 24.7 %all-gather.2.cloned.1.call-done = f32[8,4,64,256]{3,2,1,0:T(8,128)} async-done(((f32[8,1,64,256]{3,2,1,0:T(8,128)}), f32[8,4,64,256]{3,2,1,0:T(8,128)}) %all-gather.2.cloned.1.call-update) | async-done | bytes 2097168 | tf_op jit(solution)/shard_map/all_gather | solution.py:63
  32.0 10.3 %convolution_bitcast_fusion = f32[8,4,8,64,64]{3,4,2,0,1:T(8,128)} fusion(f32[4,8,64,256,1]{3,2,4,1,0:T(8,128)} %bitcast.130, f32[8,1,64,256]{3,2,1,0:T(8,128)} %param.11), kind=kOutput, calls=%fused_computation.9 | convolution fusion | flops 3221225472 | bytes 6815744 | tf_op jit(solution)/shard_map/trp,scup->cstru/dot_general | solution.py:66
  42.3 9.2 %copy.46 = f32[8,4,8,64,64]{4,3,2,1,0:T(8,128)} copy(f32[8,4,8,64,64]{3,4,2,0,1:T(8,128)} %convolution_bitcast_fusion) | data formatting | bytes 8388608 | tf_op jit(solution)/shard_map/trp,scup->cstru/transpose | solution.py:66
  51.4 7.9 %reshape.481 = f32[32,8,4096]{2,1,0:T(8,128)} reshape(f32[8,4,8,64,64]{4,3,2,1,0:T(8,128)} %copy.46) | data formatting | bytes 8388608 | tf_op jit(solution)/shard_map/reshape | solution.py:74
  59.4 0.3 all-reduce.5.cloned.1.call-start
  59.7 0.5 copy-done.5
  60.3 0.7 fusion.32
  61.1 0.2 select_reduce_fusion.3
  61.2 0.2 select_reduce_fusion
  61.6 1.9 copy.44
  63.5 0.2 select_reduce_fusion.4
  63.9 84.0 %reduce-scatter.2.cloned.1.call-done = f32[4,8,4096]{2,1,0:T(8,128)} async-done(((f32[32,8,4096]{2,1,0:T(8,128)}), f32[4,8,4096]{2,1,0:T(8,128)}) %reduce-scatter.2.cloned.1.call-update) | async-done | bytes 524304 | tf_op jit(solution)/shard_map/reduce_scatter | solution.py:73
  148.0 2.4 reshape.482
  150.4 4.1 fusion.28
  154.5 25.9 %all-reduce.5.cloned.1.call-done = f32[4,64,128]{2,1,0:T(8,128)} async-done(((f32[4,64,128]{2,1,0:T(8,128)}), f32[4,64,128]{2,1,0:T(8,128)}) %all-reduce.5.cloned.1.call-update) | async-done | bytes 131088 | tf_op jit(solution)/shard_map/psum | solution.py:14
  180.4 4.6 fusion.13
  185.0 2.0 copy.48
  187.0 4.0 fusion.11
  191.1 6.5 %all-to-all-start = ((f32[4,2,4,128,128]{4,1,3,2,0:T(2,128)}), f32[4,2,4,128,128]{4,1,3,2,0:T(2,128)S(1)}, u32[]{:S(2)}, u32[]{:S(2)}) async-start(f32[4,2,4,128,128]{4,1,3,2,0:T(2,128)} %fusion.11), calls=%async_computation.1 | async-start | bytes 4194304 | tf_op jit(solution)/shard_map/all_to_all | solution.py:110
  197.6 23.8 %all-to-all-done = f32[4,2,4,128,128]{4,1,3,2,0:T(2,128)S(1)} async-done(((f32[4,2,4,128,128]{4,1,3,2,0:T(2,128)}), f32[4,2,4,128,128]{4,1,3,2,0:T(2,128)S(1)}, u32[]{:S(2)}, u32[]{:S(2)}) %all-to-all-start) | async-done | bytes 2097184 | tf_op jit(solution)/shard_map/all_to_all | solution.py:110
  221.3 3.3 fusion.20
  224.6 3.6 fusion.16
  228.2 2.8 copy.51
  231.0 5.5 all-to-all-start.1
  236.5 0.6 all-reduce.9.cloned.1.call-start
  237.8 0.2 select_reduce_fusion.1
  238.0 0.2 select_reduce_fusion.2
  238.2 87.7 %all-to-all-done.1 = f32[8,8,128,128]{3,2,1,0:T(8,128)} async-done(((f32[8,8,128,128]{3,2,1,0:T(8,128)}), f32[8,8,128,128]{3,2,1,0:T(8,128)}, u32[]{:S(2)}, u32[]{:S(2)}) %all-to-all-start.1) | async-done | bytes 4194336 | tf_op jit(solution)/shard_map/all_to_all | solution.py:128
  325.9 6.4 %fusion.23 = f32[8,4,128,128]{3,1,2,0:T(4,128)S(1)} fusion(f32[8,8,128,128]{3,2,1,0:T(8,128)} %all-to-all-done.1, s32[4]{0:T(128)S(1)} %get-tuple-element.10), kind=kOutput, calls=%fused_computation.25 | convolution fusion | flops 50331680 | bytes 6291472 | tf_op jit(solution)/shard_map/sq,qtxy->tsxy/dot_general | solution.py:131
  332.4 2.8 fusion.14
  335.2 13.2 %bitcast_add_fusion = f32[16,8,128,128]{3,1,2,0:T(8,128)S(1)} fusion(f32[16,1,8,1,128,128]{5,4,3,2,1,0:T(8,128)} %param.9, f32[16,4,128,128]{3,0,2,1:T(8,128)S(1)} %fusion.14, s32[4]{0:T(128)S(1)} %and_select_fusion), kind=kOutput, calls=%fused_computation.2 | convolution fusion | flops 102760480 | bytes 20971536 | tf_op jit(solution)/shard_map/bs,asxy->abxy/dot_general | solution.py:153
  348.4 1.3 broadcast.600
  349.6 7.2 %broadcast_select_fusion = (f32[16,1,128,128]{3,1,2,0:T(1,128)}, f32[16,1,128,128]{3,1,2,0:T(1,128)S(1)}, f32[16,1,128,128]{3,1,2,0:T(1,128)S(1)}, f32[16,1,128,128]{3,1,2,0:T(1,128)S(1)}) fusion(f32[16,1,128,128]{3,1,2,0:T(1,128)} %bitcast.134, pred[]{:T(512)S(6)} %eq.267, f32[16,8,128,128]{3,1,2,0:T(8,128)S(1)} %bitcast_add_fusion, s32[]{:T(128)S(6)} %select_n.288, ...), kind=kLoop, calls=%fused_computation.23 | loop fusion | flops 262144 | bytes 9437201 | tf_op jit(solution)/shard_map/jit(_where)/select_n | solution.py:14
  356.8 1.1 select_bitcast_fusion.2
  357.9 1.6 select_bitcast_fusion
  359.6 158.4 %all-reduce.9.cloned.1.call-done = (f32[16,128,128]{2,1,0:T(8,128)}, f32[16,128,128]{2,1,0:T(8,128)}, f32[16,128,128]{2,1,0:T(8,128)}, f32[16,128,128]{2,1,0:T(8,128)}) async-done(((f32[16,128,128]{2,1,0:T(8,128)}, f32[16,128,128]{2,1,0:T(8,128)}, f32[16,128,128]{2,1,0:T(8,128)}, f32[16,128,128]{2,1,0:T(8,128)}), (f32[16,128,128]{2,1,0:T(8,128)}, f32[16,128,128]{2,1,0:T(8,128)}, f32[16,128,128]{2,1,0:T(8,128)}, ...) | async-done | bytes 4194320 | tf_op jit(solution)/shard_map/psum | solution.py:14
  518.0 1.5 constant_dynamic-update-slice_fusion.3
  519.5 1.4 constant_dynamic-update-slice_fusion.2
  520.8 0.1 constant_dynamic-update-slice_fusion.1
  521.1 1.9 copy-done.2
  523.1 1.6 fusion.9
  524.8 10.1 %fusion.26 = f32[16,128,512]{2,1,0:T(8,128)} fusion(f32[16,128,512]{2,1,0:T(8,128)} %copy-done.2, f32[512,512]{1,0:T(8,128)S(1)} %copy-done), kind=kOutput, calls=%fused_computation.26 | convolution fusion | flops 6442450944 | bytes 9437184 | tf_op jit(solution)/shard_map/axp,pq->axq/dot_general | solution.py:165
  534.9 40.6 %all-reduce.7.cloned.1.call-done = f32[8,128,512]{2,1,0:T(8,128)} async-done(((f32[8,128,512]{2,1,0:T(8,128)}), f32[8,128,512]{2,1,0:T(8,128)}) %all-reduce.7.cloned.1.call-update) | async-done | bytes 2097168 | tf_op jit(solution)/shard_map/psum | solution.py:14
  575.5 18.0 %fusion.1 = f32[8,128,16,128]{3,1,2,0:T(8,128)} fusion(f32[16,128,512]{2,1,0:T(8,128)} %fusion.26, f32[8,128,512]{2,1,0:T(8,128)} %all-reduce.7.cloned.1.call-done), kind=kOutput, calls=%fused_computation.3 | convolution fusion | flops 12884901888 | bytes 14680064 | tf_op jit(solution)/shard_map/axq,byq->abxy/dot_general | solution.py:172
  593.4 9.5 %copy.60 = f32[8,128,16,128]{1,0,3,2:T(8,128)} copy(f32[8,128,16,128]{3,1,2,0:T(8,128)} %fusion.1) | data formatting | bytes 16777216 | tf_op jit(solution)/shard_map/axq,byq->abxy/dot_general | solution.py:172
  602.9 10.1 %fusion = f32[16,1,8,1,128,128]{5,2,4,0,3,1:T(8,128)} fusion(f32[16,8,128,128]{3,1,2,0:T(8,128)} %copy-done.1, f32[8,128,16,128]{1,0,3,2:T(8,128)} %copy.60, pred[16,8]{1,0:T(8,128)(4,1)S(1)} %compare_and_fusion), kind=kLoop, calls=%fused_computation.1 | loop fusion | flops 4194304 | bytes 25165952 | tf_op jit(solution)/shard_map/broadcast_in_dim | solution.py:179
  613.1 8.2 %copy.61 = f32[16,1,8,1,128,128]{5,4,3,2,1,0:T(8,128)} copy(f32[16,1,8,1,128,128]{5,2,4,0,3,1:T(8,128)} %fusion) | data formatting | bytes 16777216 | tf_op jit(solution)/shard_map/broadcast_in_dim | solution.py:179
  (44 shorter events, 0.9 us)
Async XLA Ops:
  6.5 518.3 %copy-start = (f32[512,512]{1,0:T(8,128)S(1)}, f32[512,512]{1,0:T(8,128)}, u32[]{:S(2)}) copy-start(f32[512,512]{1,0:T(8,128)} %param.15) | copy-start | bytes 3145732
  6.5 25.4 %all-gather.2.cloned.1.call-start = ((), (), s32[]{:S(2)}) async-start(), calls=%async_computation.4 | async-start | bytes 2621440 | tf_op jit(solution)/shard_map/all_gather | solution.py:63
  7.3 140.7 %reduce-scatter.2.cloned.1.call-start = ((), (), s32[]{:S(2)}) async-start(), calls=%async_computation.5 | async-start | bytes 4718592 | tf_op jit(solution)/shard_map/reduce_scatter | solution.py:73
  59.3 0.9 copy-start.5
  59.3 1.7 copy-start.6
  59.3 4.2 copy-start.7
  59.4 121.0 %all-reduce.5.cloned.1.call-start = ((), (), s32[]{:S(2)}) async-start(), calls=%async_computation.3 | async-start | bytes 262144 | tf_op jit(solution)/shard_map/psum | solution.py:14
  191.1 30.3 %all-to-all-start = ((f32[4,2,4,128,128]{4,1,3,2,0:T(2,128)}), f32[4,2,4,128,128]{4,1,3,2,0:T(2,128)S(1)}, u32[]{:S(2)}, u32[]{:S(2)}) async-start(f32[4,2,4,128,128]{4,1,3,2,0:T(2,128)} %fusion.11), calls=%async_computation.1 | async-start | bytes 4194304 | tf_op jit(solution)/shard_map/all_to_all | solution.py:110
  231.0 94.9 %all-to-all-start.1 = ((f32[8,8,128,128]{3,2,1,0:T(8,128)}), f32[8,8,128,128]{3,2,1,0:T(8,128)}, u32[]{:S(2)}, u32[]{:S(2)}) async-start(f32[8,8,128,128]{3,2,1,0:T(8,128)} %copy.51), calls=%async_computation.2 | async-start | bytes 8388608 | tf_op jit(solution)/shard_map/all_to_all | solution.py:128
  236.5 281.5 %all-reduce.9.cloned.1.call-start = ((), (), s32[]{:S(2)}) async-start(), calls=%async_computation.7 | async-start | bytes 8388608 | tf_op jit(solution)/shard_map/psum | solution.py:14
  348.4 8.5 %copy-start.1 = (f32[16,8,128,128]{3,1,2,0:T(8,128)}, f32[16,8,128,128]{3,1,2,0:T(8,128)S(1)}, u32[]{:S(2)}) copy-start(f32[16,8,128,128]{3,1,2,0:T(8,128)S(1)} %bitcast_add_fusion) | copy-start | bytes 25165828
  359.5 215.9 %all-reduce.7.cloned.1.call-start = ((), (), s32[]{:S(2)}) async-start(), calls=%async_computation.6 | async-start | bytes 4194304 | tf_op jit(solution)/shard_map/psum | solution.py:14
  518.0 2.9 copy-start.4
  518.0 3.0 copy-start.3
  521.1 2.0 copy-start.2
Sparse Core Ops, SparseCore 0:
  8.9 23.0 all-gather.1
  59.5 88.4 reduce-scatter.1
  150.3 30.0 all-reduce.4
  359.7 158.2 all-reduce.8
  524.8 50.6 all-reduce.6
where the time goes:
time: 636 us; the launch traced here: 628 us
  waiting for transfers between devices  446 us (70%)
  matrix products  80.4 us (13%)
  local copies, waits for them, and re-layouts  51 us (8%)
  other arithmetic  23.6 us (4%)
  between operations  14.5 us (2%)
  starting transfers between devices  12.9 us (2%)
    psum x3, waiting for transfers between devices, spread_2(): return lax.psum(jnp.where(mine, x, jnp.zeros_like(x)), axis)  225 us
    all_to_all x1, waiting for transfers between devices, per_device(): lax.all_to_all(packed, 'col', split_axis=0, concat_axis=0, tiled=True)  87.7 us
    reduce_scatter x1, waiting for transfers between devices, per_device(): lax.psum_scatter(products.reshape(lax.axis_size('col') * local_cols, loca...  84 us
    all_gather x1, waiting for transfers between devices, per_device(): all_pivots = lax.all_gather(pivot_basis, 'row', axis=1, tiled=True)  24.7 us
    all_to_all x1, waiting for transfers between devices, per_device(): lax.all_to_all(packed, 'row', split_axis=0, concat_axis=0, tiled=True)  23.8 us
    dot_general x1, matrix products, per_device(): jnp.einsum('axq,byq->abxy', scaled, col_panel, precision=highest, preferr...  18 us
    dot_general x1, matrix products, per_device(): jnp.einsum('bs,asxy->abxy', col_place, spread, precision=highest, preferr...  13.2 us
  transfers between devices with their start and end apart: 7, of which 7 were waited for; matrix products, arithmetic and copies ran while one was open for 3% of the time, Pallas kernels for 0%

commit v1 on v0

v1 whole, which is shorter than its diff:
```python
import jax
import jax.numpy as jnp
from jax import lax
from jax.experimental import pallas as pl
from jax.experimental.pallas import tpu as pltpu
from jax.sharding import PartitionSpec as P

PANEL_T = 4
f32 = jnp.float32
bf16 = jnp.bfloat16
high = lax.Precision.HIGH


def rotate(x, axis, amount):
    n = lax.axis_size(axis)

    def branch(k):
        pairs = [(d, (d + k) % n) for d in range(n)]
        return (lambda v: v) if k == 0 else (lambda v: lax.ppermute(v, axis, pairs))

    return lax.switch(amount, [branch(k) for k in range(n)], x)


def gather_ring(x, axis):
    return lax.all_gather(x, axis, axis=0, tiled=False)


def split(x):
    top = x.astype(bf16)
    return top, (x - top.astype(f32)).astype(bf16)


def split_outside(x):
    top = lax.reduce_precision(x, exponent_bits=8, mantissa_bits=7)
    return top.astype(bf16), (x - top).astype(bf16)


def dot3(a, b, dims):
    (ah, al), (bh, bl) = a, b
    one = lambda p, q: lax.dot_general(p, q, (dims, ((), ())), preferred_element_type=f32)
    return one(ah, bh) + (one(ah, bl) + one(al, bh))


def final_kernel(table, parent, payload, panel, inv_top, inv_low, col_top, col_low, out):
    row = pl.program_id(0)
    bcols = parent.shape[2]
    tile = parent.shape[4]
    blocks = payload.shape[0]
    row_panel = jnp.concatenate([panel[0, 0, m, 0] for m in range(panel.shape[2])], axis=1)
    scaled = dot3(split(row_panel), (inv_top[...], inv_low[...]), ((1,), (0,)))
    trailing = dot3(split(scaled), (col_top[...], col_low[...]), ((1,), (1,)))
    big_row = table[0, 0] + row * table[0, 1]
    place = table[1, row]
    from_row = jnp.maximum(place, 0)
    for b in range(bcols):
        big_col = table[0, 2] + b * table[0, 3]
        s = b // (bcols // blocks)
        hit = (place >= 0) & (table[2, b] > 0)
        active = (big_row >= big_col) & (big_col >= table[0, 4])
        base = parent[0, 0, b, 0] + jnp.where(hit, payload[s, from_row], 0.0)
        out[0, 0, b, 0] = base - jnp.where(active, trailing[:, b * tile : (b + 1) * tile], 0.0)


def finish(table, parent, payload, panel, inv, cols):
    rows, _, bcols, _, tile, _ = parent.shape
    parities, subs, width, piece = panel.shape[:4]
    whole = lambda a: pl.BlockSpec(a.shape, lambda i, t: (0,) * a.ndim)
    big = pl.BlockSpec((1, 1, bcols, 1, tile, tile), lambda i, t: (i, 0, 0, 0, 0, 0))
    picked = pl.BlockSpec(
        (1, 1, width, 1, tile, tile),
        lambda i, t: (i % parities, i // parities // piece, 0, i // parities % piece, 0, 0),
    )
    flops = 6 * rows * tile * width * tile * (width + bcols) * tile
    return pl.pallas_call(
        final_kernel,
        grid_spec=pltpu.PrefetchScalarGridSpec(
            num_scalar_prefetch=1,
            grid=(rows,),
            in_specs=[big, whole(payload), picked, whole(inv[0]), whole(inv[1]), whole(cols[0]), whole(cols[1])],
            out_specs=big,
        ),
        out_shape=jax.ShapeDtypeStruct(parent.shape, f32),
        cost_estimate=pl.CostEstimate(flops=flops, bytes_accessed=10 * parent.size, transcendentals=0),
    )(table, parent, payload, panel, *inv, *cols)


def per_device(
    contribution,
    parent_tiles,
    row_basis,
    pivot_basis,
    tile_ranks,
    block_map,
    panel_start,
    pivot_inverse,
):
    R = lax.axis_size("row")
    C = lax.axis_size("col")
    my_row = lax.axis_index("row")
    my_col = lax.axis_index("col")
    T, S = contribution.shape[0], contribution.shape[2]
    tile = contribution.shape[4]
    rows, bcols = parent_tiles.shape[0], parent_tiles.shape[2]
    rank = row_basis.shape[2]
    width = pivot_basis.shape[3]
    per = C // R
    span = rows // S
    shift = [block_map[u * C] - 2 * u * C for u in range(S)]
    src_row = [(my_row - shift[u]) % R for u in range(S)]
    src_col = [(my_col - shift[s]) % C for s in range(S)]

    child = contribution[:, 0, :, 0]
    by_row = [rotate(child[u * per : (u + 1) * per, : u + 1], "row", shift[u] % R) for u in range(S)]
    moved = [
        rotate(jnp.concatenate([by_row[u][:, s] for u in range(s, S)], axis=0), "col", shift[s])
        for s in range(S)
    ]

    factors = jnp.concatenate([pivot_basis[:, 0], row_basis[:, 0]], axis=2)
    everyone = gather_ring(factors, "row")
    pivots = everyone[..., :width]
    limits = tile_ranks.reshape(T, R).T
    kept = jnp.arange(rank, dtype=jnp.int32)[None, None, :] < limits[:, :, None]
    bases = everyone[..., width:] * kept[..., None].astype(f32)

    def of_rows(stack, u):
        return lax.dynamic_index_in_dim(stack, src_row[u], axis=0, keepdims=False)[u * per : (u + 1) * per]

    pivot_rows = [of_rows(pivots, u).reshape(per * rank, width) for u in range(S)]
    basis_rows = [of_rows(bases, u) for u in range(S)]
    flat_bases = jnp.swapaxes(bases, 0, 1).reshape(S, C, rank, tile)
    flat_pivots = jnp.swapaxes(pivots, 0, 1).reshape(S, C, rank, width)
    partial = []
    for s in range(S):
        mine = jnp.concatenate(pivot_rows[s:], axis=0)
        theirs = jnp.roll(flat_pivots[s], shift[s], axis=0)
        partial.append(jnp.einsum("cqp,mp->cqm", theirs, mine, precision=high, preferred_element_type=f32))
    partial = jnp.concatenate(partial, axis=2)
    weights = lax.psum_scatter(partial, "col", scatter_dimension=0, tiled=True)[0]

    payload, at = [], 0
    for s in range(S):
        size = (S - s) * per * rank
        basis_col = lax.dynamic_index_in_dim(flat_bases[s], src_col[s], axis=0, keepdims=False)
        half = jnp.einsum("qm,qy->my", weights[:, at : at + size], basis_col, precision=high, preferred_element_type=f32)
        at += size
        half = half.reshape((S - s) * per, rank, tile)
        left = jnp.concatenate(basis_rows[s:], axis=0)
        update = jnp.einsum("trx,try->txy", left, half, precision=high, preferred_element_type=f32)
        i = jnp.stack([(u * per + p) * R + src_row[u] for u in range(s, S) for p in range(per)])
        j = s * C + src_col[s]
        tiles = jnp.where((i >= j)[:, None, None], moved[s] - update, 0.0)
        payload.append(jnp.concatenate([jnp.zeros((s * per, tile, tile), f32), tiles], axis=0))
    payload = jnp.stack(payload)

    first_row = jnp.stack([(2 * u * C + shift[u] + src_row[u]) // R for u in range(S)])
    a = jnp.arange(rows, dtype=jnp.int32)
    u_of = a // span
    p_of = a - first_row[u_of]
    place = jnp.where((p_of >= 0) & (p_of < per), u_of * per + p_of, -1).astype(jnp.int32)
    target_col = jnp.stack([(2 * s * C + shift[s] + src_col[s]) // C for s in range(S)])
    b = jnp.arange(bcols, dtype=jnp.int32)
    col_hit = (target_col[b // (bcols // S)] == b).astype(jnp.int32)

    start = panel_start[0]
    owned = (my_col - start) % C < PANEL_T
    own_b = jnp.minimum((start + (my_col - start) % C) // C, bcols - 1)
    column = lax.dynamic_index_in_dim(parent_tiles[:, 0, :, 0], own_b, axis=1, keepdims=False)
    extra = lax.dynamic_index_in_dim(payload, own_b // (bcols // S), axis=0, keepdims=False)
    extra = extra.reshape(S, per, tile, tile)
    grouped = place.reshape(S, span)
    spread = jnp.zeros((S, span, tile, tile), f32)
    for p in range(per):
        sel = (grouped == jnp.arange(S, dtype=jnp.int32)[:, None] * per + p)[:, :, None, None]
        spread = spread + jnp.where(sel, extra[:, p][:, None], 0.0)
    hit = lax.dynamic_index_in_dim(col_hit, own_b, axis=0, keepdims=False) > 0
    column = column + jnp.where(hit, spread.reshape(rows, tile, tile), 0.0)
    subs = R // PANEL_T
    piece = rows // per // subs
    pieces = column.reshape(subs, piece, per, tile, tile)
    pieces = jnp.moveaxis(pieces, 2, 0).reshape(per * subs, piece, tile, tile)
    members = C // PANEL_T
    my_member = my_col // PANEL_T
    held = lax.dynamic_index_in_dim(pieces, my_member, axis=0, keepdims=False)
    for k in range(1, members):
        gone = lax.dynamic_index_in_dim(pieces, (my_member + k) % members, axis=0, keepdims=False)
        came = lax.ppermute(gone, "col", [(d, (d + PANEL_T * k) % C) for d in range(C)])
        theirs = (my_col - PANEL_T * k - start) % C < PANEL_T
        held = jnp.where(theirs, came, held)
    panel = gather_ring(held, "col").reshape(per, subs, PANEL_T, piece, tile, tile)
    cols = lax.dynamic_index_in_dim(panel, my_col // R, axis=0, keepdims=False)
    cols = lax.psum(jnp.where(my_row == my_col % R, cols, 0.0), "row")
    cols = jnp.transpose(cols, (0, 2, 3, 1, 4)).reshape(bcols * tile, PANEL_T * tile)
    inverse = pivot_inverse.reshape(PANEL_T, tile, PANEL_T, tile)
    inverse = jnp.roll(inverse, (start % PANEL_T, start % PANEL_T), axis=(0, 2))
    inverse = inverse.reshape(PANEL_T * tile, PANEL_T * tile)
    scalars = jnp.stack([my_row, R + 0 * my_row, my_col, C + 0 * my_row, start + PANEL_T]).astype(jnp.int32)
    pad = lambda v: jnp.concatenate([v, jnp.zeros((rows - v.shape[0],), jnp.int32)])
    table = jnp.stack([pad(scalars), place, pad(col_hit)])
    return finish(table, parent_tiles, payload, panel, split_outside(inverse), split_outside(cols))


def solution(mesh):
    placed = (
        P(None, "row", None, "col", None, None),
        P(None, "row", None, "col", None, None),
        P(None, "row", None, None),
        P(None, "row", None, "col"),
        P(),
        P(),
        P(),
        P(),
    )
    return jax.shard_map(
        per_device,
        mesh=mesh,
        in_specs=placed,
        out_specs=P(None, "row", None, "col", None, None),
        check_vma=False,
    )
```

time: 636 us -> 352 us (0.55); the launches traced: 628 us -> 353 us
  waiting for transfers between devices: 446 us -> 214 us
  matrix products: 80.4 us -> 7.74 us
  Pallas kernels: 0 us -> 28.6 us
  local copies, waits for them, and re-layouts: 51 us -> 31.5 us
  starting transfers between devices: 12.9 us -> 28.2 us
  between operations: 14.5 us -> 27.1 us
  other arithmetic: 23.6 us -> 16.2 us
    psum x3 -> x1, waiting for transfers between devices: 225 us -> 46.1 us  [per_device(): cols = lax.psum(jnp.where(my_row == my_col % R, cols, 0.0), 'row')]
    all_to_all x2 -> x0, waiting for transfers between devices: 111 us -> none  [the longest x1 87.7 us: per_device(): lax.all_to_all(packed, 'col', split_axis=0, concat_axis=0, tiled=True)]
    reduce_scatter x1, waiting for transfers between devices: 84 us -> 0.02 us  [per_device(): lax.psum_scatter(partial, 'col', scatter_dimension=0, tiled=True)[0]]
    dot_general x11 -> x12, matrix products: 80.4 us -> 7.74 us  [the longest x4 3.9 us: per_device(): jnp.einsum('qm,qy->my', weights[:, at:at + size], basis_col, precision=hi...]
    all_gather x1 -> x2, waiting for transfers between devices: 24.7 us -> 97.1 us  [gather_ring(): return lax.all_gather(x, axis, axis=0, tiled=False)]
    ppermute x0 -> x8, waiting for transfers between devices: none -> 70.3 us  [the longest x7 50.5 us: branch(): return (lambda v: v) if k == 0 else lambda v: lax.ppermute(v, axis, pairs)]
    pallas_call x0 -> x1, Pallas kernels: none -> 28.6 us  [finish(): pl.pallas_call(final_kernel, grid_spec=pltpu.PrefetchScalarGridSpec(num_s...]
    ppermute x0 -> x8, starting transfers between devices: none -> 28.1 us  [the longest x7 15.1 us: branch(): return (lambda v: v) if k == 0 else lambda v: lax.ppermute(v, axis, pairs)]
  transfers between devices with their start and end apart: 7 -> 12, of which waited for: 7 -> 11; matrix products, arithmetic and copies ran while one was open for 3% -> 7% of each run, Pallas kernels for 0% -> 0%
where the time goes in v1:
time: 352 us; the launch traced here: 353 us
  waiting for transfers between devices  214 us (61%)
  local copies, waits for them, and re-layouts  31.5 us (9%)
  Pallas kernels  28.6 us (8%)
  starting transfers between devices  28.2 us (8%)
  between operations  27.1 us (8%)
  other arithmetic  16.2 us (5%)
  matrix products  7.74 us (2%)
    all_gather x2, waiting for transfers between devices, gather_ring(): return lax.all_gather(x, axis, axis=0, tiled=False)  97.1 us
    ppermute x7, waiting for transfers between devices, branch(): return (lambda v: v) if k == 0 else lambda v: lax.ppermute(v, axis, pairs)  50.5 us
    psum x1, waiting for transfers between devices, per_device(): cols = lax.psum(jnp.where(my_row == my_col % R, cols, 0.0), 'row')  46.1 us
    pallas_call x1, Pallas kernels, finish(): pl.pallas_call(final_kernel, grid_spec=pltpu.PrefetchScalarGridSpec(num_s...  28.6 us
    ppermute x1, waiting for transfers between devices, per_device(): lax.ppermute(gone, 'col', [(d, (d + PANEL_T * k) % C) for d in range(C)])  19.8 us
    ppermute x7, starting transfers between devices, branch(): return (lambda v: v) if k == 0 else lambda v: lax.ppermute(v, axis, pairs)  15.1 us
    ppermute x1, starting transfers between devices, per_device(): lax.ppermute(gone, 'col', [(d, (d + PANEL_T * k) % C) for d in range(C)])  13 us
  transfers between devices with their start and end apart: 12, of which 11 were waited for; matrix products, arithmetic and copies ran while one was open for 7% of the time, Pallas kernels for 0%

profile of v1, /device:TPU:21, one launch (start us, length us, event | category | flops | bytes accessed | tf_op | source)
XLA Modules:
  0.0 353.4 jit_solution(11843376707847063970)
XLA Ops:
  6.5 2.1 pad_maximum_fusion.2
  14.2 23.7 %all-gather.5.cloned.1.call-done = f32[32,64,384]{2,1,0:T(8,128)} async-done(((f32[8,64,384]{2,1,0:T(8,128)}), f32[32,64,384]{2,1,0:T(8,128)}) %all-gather.5.cloned.1.call-update) | async-done | bytes 3145744 | tf_op jit(solution)/shard_map/all_gather | solution.py:25
  37.9 2.1 slice_bitcast_fusion.21
  42.5 1.7 pad_maximum_fusion
  55.1 5.0 %conditional.8 = (f32[2,128,128]{2,1,0:T(8,128)}) conditional(s32[]{:T(128)} %clamp.25, f32[8,4,128,128]{3,2,1,0:T(8,128)S(1)} %bitcast.222, f32[8,4,128,128]{3,2,1,0:T(8,128)S(1)} %bitcast.223, f32[8,4,128,128]{3,2,1,0:T(8,128)S(1)} %bitcast.224, f32[8,4,128,128]{3,2,1,0:T(8,128)S(1)} %bitcast.225), branch_computations={%region_0.1_spmd, %region_1.2_spmd, %region_2.3_spmd, %region_3.4_... | conditional | bytes 786480 | solution.py:21
  55.1 1.3 collective-permute-start.32
  56.4 3.7 %collective-permute-done.32 = f32[2,1,128,128]{3,2,0,1:T(8,128)} collective-permute-done((f32[2,1,128,128]{3,2,0,1:T(8,128)S(1)}, f32[2,1,128,128]{3,2,0,1:T(8,128)}, u32[]{:S(2)}, u32[]{:S(2)}) %collective-permute-start.32) | collective-permute-done | bytes 131104 | tf_op jit(solution)/shard_map/cond/branch_2_fun/ppermute | solution.py:19
  60.1 10.0 %conditional.9 = (f32[2,2,128,128]{3,2,1,0:T(8,128)}, f32[2,1,128,128]{3,2,1,0:T(8,128)}, f32[2,1,128,128]{3,2,1,0:T(8,128)}, f32[2,128,128]{2,1,0:T(8,128)S(1)}, f32[2,128,128]{2,1,0:T(8,128)S(1)}) conditional(s32[]{:T(128)} %clamp.26, f32[8,4,128,128]{3,2,1,0:T(8,128)S(1)} %bitcast.226, ...), branch_computations={%region_4.5_spmd, %region_5.6_spmd, %region_6.7_spmd, %region_7.8_... | conditional | bytes 2621520 | solution.py:21
  60.1 1.2 collective-permute-start.39
  61.3 5.2 %collective-permute-done.39 = f32[2,2,128,128]{3,2,1,0:T(8,128)} collective-permute-done((f32[2,2,128,128]{3,2,1,0:T(8,128)S(1)}, f32[2,2,128,128]{3,2,1,0:T(8,128)}, u32[]{:S(2)}, u32[]{:S(2)}) %collective-permute-start.39) | collective-permute-done | bytes 262176 | tf_op jit(solution)/shard_map/cond/branch_3_fun/ppermute | solution.py:19
  66.5 1.7 fusion.83
  68.2 0.9 copy.195
  69.1 0.9 copy.196
  73.2 4.8 %conditional.10 = (f32[2,3,128,128]{3,2,1,0:T(8,128)}) conditional(s32[]{:T(128)} %clamp.27, (f32[8,4,128,128]{3,2,1,0:T(8,128)S(1)}) %tuple.261, (f32[8,4,128,128]{3,2,1,0:T(8,128)S(1)}) %tuple.262, (f32[8,4,128,128]{3,2,1,0:T(8,128)S(1)}) %tuple.263, (f32[8,4,128,128]{3,2,1,0:T(8,128)S(1)}) %tuple.264), branch_computations={%region_8.9_spmd, %region_9.10_spmd, %region_10.11_spmd, %region_1... | conditional | bytes 2359344 | solution.py:21
  73.3 4.7 %collective-permute-done = f32[2,3,128,128]{3,2,1,0:T(8,128)} collective-permute-done((f32[2,3,128,128]{3,2,1,0:T(8,128)S(1)}, f32[2,3,128,128]{3,2,1,0:T(8,128)}, u32[]{:S(2)}, u32[]{:S(2)}) %collective-permute-start) | collective-permute-done | bytes 393248 | tf_op jit(solution)/shard_map/cond/branch_1_fun/ppermute | solution.py:19
  78.0 0.8 conditional.11
  78.9 1.3 slice_bitcast_fusion.16
  80.2 4.9 %conditional.15 = (f32[2,128,128]{2,1,0:T(8,128)S(1)}) conditional(s32[]{:T(128)} %clamp.31, f32[2,128,128]{2,1,0:T(8,128)S(1)} %get-tuple-element.176, f32[2,128,128]{2,1,0:T(8,128)S(1)} %get-tuple-element.176, f32[2,128,128]{2,1,0:T(8,128)S(1)} %get-tuple-element.176, ...), branch_computations={%region_41.43_spmd, %region_42.44_spmd, %region_43.45_spmd, %regio... | conditional | bytes 786480 | solution.py:21
  80.8 4.4 %collective-permute-done.27 = f32[2,128,128]{2,1,0:T(8,128)S(1)} collective-permute-done((f32[2,128,128]{2,1,0:T(8,128)S(1)}, f32[2,128,128]{2,1,0:T(8,128)S(1)}, u32[]{:S(2)}, u32[]{:S(2)}) %collective-permute-start.27) | collective-permute-done | bytes 131104 | tf_op jit(solution)/shard_map/cond/branch_4_fun/ppermute | solution.py:19
  85.8 8.2 %conditional.14 = (f32[4,128,128]{2,1,0:T(8,128)S(1)}) conditional(s32[]{:T(128)} %clamp.30, f32[4,128,128]{2,1,0:T(8,128)S(1)} %pad_maximum_fusion.5, f32[4,128,128]{2,1,0:T(8,128)S(1)} %pad_maximum_fusion.5, f32[4,128,128]{2,1,0:T(8,128)S(1)} %pad_maximum_fusion.5, ...), branch_computations={%region_33.35_spmd, %region_34.36_spmd, %region_35.37_spmd, %regio... | conditional | bytes 1572912 | solution.py:21
  85.9 1.5 collective-permute-start.17
  87.4 6.6 %collective-permute-done.17 = f32[4,128,128]{2,1,0:T(8,128)S(1)} collective-permute-done((f32[4,128,128]{2,1,0:T(8,128)S(1)}, f32[4,128,128]{2,1,0:T(8,128)S(1)}, u32[]{:S(2)}, u32[]{:S(2)}) %collective-permute-start.17) | collective-permute-done | bytes 262176 | tf_op jit(solution)/shard_map/cond/branch_1_fun/ppermute | solution.py:19
  94.0 1.0 pad_maximum_fusion.3
  95.1 18.9 %conditional.12 = (f32[8,128,128]{2,1,0:T(8,128)S(1)}) conditional(s32[]{:T(128)} %clamp.24, f32[8,128,128]{2,1,0:T(8,128)S(1)} %pad_maximum_fusion.3, f32[8,128,128]{2,1,0:T(8,128)S(1)} %pad_maximum_fusion.3, f32[8,128,128]{2,1,0:T(8,128)S(1)} %pad_maximum_fusion.3, ...), branch_computations={%region_16.17_spmd, %region_17.18_spmd, %region_18.19_spmd, %regio... | conditional | bytes 3145776 | solution.py:21
  95.2 18.8 %collective-permute-done.8 = f32[8,128,128]{2,1,0:T(8,128)S(1)} collective-permute-done((f32[8,128,128]{2,1,0:T(8,128)S(1)}, f32[8,128,128]{2,1,0:T(8,128)S(1)}, u32[]{:S(2)}, u32[]{:S(2)}) %collective-permute-start.8) | collective-permute-done | bytes 524320 | tf_op jit(solution)/shard_map/cond/branch_6_fun/ppermute | solution.py:19
  114.9 17.8 %conditional.13 = (f32[6,128,128]{2,1,0:T(8,128)S(1)}) conditional(s32[]{:T(128)} %clamp.29, f32[6,128,128]{2,1,0:T(8,128)S(1)} %pad_maximum_fusion.4, f32[6,128,128]{2,1,0:T(8,128)S(1)} %pad_maximum_fusion.4, f32[6,128,128]{2,1,0:T(8,128)S(1)} %pad_maximum_fusion.4, ...), branch_computations={%region_25.27_spmd, %region_26.28_spmd, %region_27.29_spmd, %regio... | conditional | bytes 2359344 | solution.py:21
  114.9 10.4 %collective-permute-start.12 = (f32[6,128,128]{2,1,0:T(8,128)S(1)}, f32[6,128,128]{2,1,0:T(8,128)S(1)}, u32[]{:S(2)}, u32[]{:S(2)}) collective-permute-start(f32[6,128,128]{2,1,0:T(8,128)S(1)} %param.29), channel_id=1, source_target_pairs={{0,3},{1,4},{2,5},{3,6},{4,7},{5,0},{6,1},{7,2},{8,11},{9,12},{10,... | collective-permute-start | bytes 1179656 | tf_op jit(solution)/shard_map/cond/branch_3_fun/ppermute | solution.py:19
  125.4 7.1 %collective-permute-done.12 = f32[6,128,128]{2,1,0:T(8,128)S(1)} collective-permute-done((f32[6,128,128]{2,1,0:T(8,128)S(1)}, f32[6,128,128]{2,1,0:T(8,128)S(1)}, u32[]{:S(2)}, u32[]{:S(2)}) %collective-permute-start.12) | collective-permute-done | bytes 393248 | tf_op jit(solution)/shard_map/cond/branch_3_fun/ppermute | solution.py:19
  132.9 2.4 constant_dynamic-slice_fusion.1
  141.7 0.9 slice_bitcast_fusion.18
  142.6 0.9 slice_bitcast_fusion.15
  143.9 1.0 fusion.52
  145.6 1.0 fusion.50
  147.1 0.9 fusion.48
  148.4 1.0 fusion.54
  150.4 1.8 copy-done.2
  152.5 13.0 %collective-permute-start.40 = (f32[8,128,128]{2,1,0:T(8,128)S(1)}, f32[8,128,128]{2,1,0:T(8,128)S(1)}, u32[]{:S(2)}, u32[]{:S(2)}) collective-permute-start(f32[8,128,128]{2,1,0:T(8,128)S(1)} %dynamic-slice_bitcast_fusion), channel_id=1, source_target_pairs={{0,4},{1,5},{2,6},{3,7},{4,0},{5,1},{6,2},{7,3},{8,12},{9,13},{10,... | collective-permute-start | bytes 1572872 | tf_op jit(solution)/shard_map/ppermute | solution.py:187
  165.6 19.8 %collective-permute-done.40 = f32[8,128,128]{2,1,0:T(8,128)S(1)} collective-permute-done((f32[8,128,128]{2,1,0:T(8,128)S(1)}, f32[8,128,128]{2,1,0:T(8,128)S(1)}, u32[]{:S(2)}, u32[]{:S(2)}) %collective-permute-start.40) | collective-permute-done | bytes 524320 | tf_op jit(solution)/shard_map/ppermute | solution.py:187
  185.4 0.9 bitcast_select_fusion
  186.3 73.4 %all-gather.7.cloned.1.call-done = f32[64,128,128]{2,1,0:T(8,128)} async-done(((f32[8,128,128]{2,1,0:T(8,128)}), f32[64,128,128]{2,1,0:T(8,128)}) %all-gather.7.cloned.1.call-update) | async-done | bytes 4194320 | tf_op jit(solution)/shard_map/all_gather | solution.py:25
  259.7 1.7 select_bitcast_fusion
  261.4 1.4 copy.92
  262.8 1.5 copy.114
  264.3 1.2 copy-done.6
  267.8 1.2 fusion.6
  268.9 46.1 %all-reduce.6.cloned.1.call-done = f32[1024,512]{1,0:T(8,128)} async-done(((f32[1024,512]{1,0:T(8,128)}), f32[1024,512]{1,0:T(8,128)}) %all-reduce.6.cloned.1.call-update) | async-done | bytes 2097168 | tf_op jit(solution)/shard_map/psum | solution.py:192
  315.0 3.3 fusion
  318.3 28.6 %shard_map.82 = f32[16,1,8,1,128,128]{5,4,3,2,1,0:T(8,128)} custom-call(s32[3,16]{1,0:T(4,128)} %pad_add_fusion.table, f32[16,1,8,1,128,128]{5,4,3,2,1,0:T(8,128)} %parent.1, f32[4,8,128,128]{3,2,1,0:T(8,128)} %copy-done.3, f32[2,1,4,8,128,128]{5,4,3,2,1,0:T(8,128)} %bitcast.262, bf16[512,512]{1,0:T(8,128)(2,1)} %get-tuple-element.162.inv_top, ...), custom_call_target="tpu_custom_call" | custom-call | flops 9663676416 | bytes 20971520 | tf_op jit(solution)/shard_map/pallas_call | solution.py:74
  (144 shorter events, 23.7 us)
Async XLA Ops:
  6.5 2.2 copy-start.11
  6.5 31.4 %all-gather.5.cloned.1.call-start = ((), (), s32[]{:S(2)}) async-start(), calls=%async_computation.3 | async-start | bytes 3932160 | tf_op jit(solution)/shard_map/all_gather | solution.py:25
  8.6 131.4 %reduce-scatter.2.cloned.1.call-start = ((), (), s32[]{:S(2)}) async-start(), calls=%async_computation.1 | async-start | bytes 2949120 | tf_op jit(solution)/shard_map/reduce_scatter | solution.py:139
  44.2 10.7 %copy-start.16 = (s32[32]{0:T(128)S(1)}, s32[32]{0:T(128)}, u32[]{:S(2)}) copy-start(s32[32]{0:T(128)} %param.62) | copy-start | bytes 388
  44.2 10.8 %copy-start = (f32[8,1,4,1,128,128]{5,4,3,2,1,0:T(8,128)S(1)}, f32[8,1,4,1,128,128]{5,4,3,2,1,0:T(8,128)}, u32[]{:S(2)}) copy-start(f32[8,1,4,1,128,128]{5,4,3,2,1,0:T(8,128)} %param.58) | copy-start | bytes 6291460
  44.2 215.5 %all-gather.7.cloned.1.call-start = ((), (), s32[]{:S(2)}) async-start(), calls=%async_computation.4 | async-start | bytes 4718592 | tf_op jit(solution)/shard_map/all_gather | solution.py:25
  55.1 5.0 %collective-permute-start.32 = (f32[2,1,128,128]{3,2,0,1:T(8,128)S(1)}, f32[2,1,128,128]{3,2,0,1:T(8,128)}, u32[]{:S(2)}, u32[]{:S(2)}) collective-permute-start(f32[2,1,128,128]{3,2,0,1:T(8,128)S(1)} %slice_bitcast_fusion.2), channel_id=1, source_target_pairs={{0,16},{8,24},{16,0},{24,8},{1,17},{9,25},{17,1},{25,9},{2,18},{10... | collective-permute-start | bytes 393224 | tf_op jit(solution)/shard_map/cond/branch_2_fun/ppermute | solution.py:19
  60.1 6.4 %collective-permute-start.39 = (f32[2,2,128,128]{3,2,1,0:T(8,128)S(1)}, f32[2,2,128,128]{3,2,1,0:T(8,128)}, u32[]{:S(2)}, u32[]{:S(2)}) collective-permute-start(f32[2,2,128,128]{3,2,1,0:T(8,128)S(1)} %slice.187), channel_id=1, source_target_pairs={{0,24},{8,0},{16,8},{24,16},{1,25},{9,1},{17,9},{25,17},{2,26},{10... | collective-permute-start | bytes 786440 | tf_op jit(solution)/shard_map/cond/branch_3_fun/ppermute | solution.py:19
  72.0 6.0 %copy-start.19 = (s32[8]{0:T(128)}, s32[8]{0:T(128)S(1)}, u32[]{:S(2)}) copy-start(s32[8]{0:T(128)S(1)} %compare_convert_fusion) | copy-start | bytes 100
  73.3 4.8 %collective-permute-start = (f32[2,3,128,128]{3,2,1,0:T(8,128)S(1)}, f32[2,3,128,128]{3,2,1,0:T(8,128)}, u32[]{:S(2)}, u32[]{:S(2)}) collective-permute-start(f32[2,3,128,128]{3,2,1,0:T(8,128)S(1)} %slice.275), channel_id=1, source_target_pairs={{0,8},{8,16},{16,24},{24,0},{1,9},{9,17},{17,25},{25,1},{2,10},{10... | collective-permute-start | bytes 1179656 | tf_op jit(solution)/shard_map/cond/branch_1_fun/ppermute | solution.py:19
  80.3 4.9 %collective-permute-start.27 = (f32[2,128,128]{2,1,0:T(8,128)S(1)}, f32[2,128,128]{2,1,0:T(8,128)S(1)}, u32[]{:S(2)}, u32[]{:S(2)}) collective-permute-start(f32[2,128,128]{2,1,0:T(8,128)S(1)} %param.46), channel_id=1, source_target_pairs={{0,4},{1,5},{2,6},{3,7},{4,0},{5,1},{6,2},{7,3},{8,12},{9,13},{10,... | collective-permute-start | bytes 393224 | tf_op jit(solution)/shard_map/cond/branch_4_fun/ppermute | solution.py:19
  85.2 0.7 copy-start.9
  85.9 8.1 %collective-permute-start.17 = (f32[4,128,128]{2,1,0:T(8,128)S(1)}, f32[4,128,128]{2,1,0:T(8,128)S(1)}, u32[]{:S(2)}, u32[]{:S(2)}) collective-permute-start(f32[4,128,128]{2,1,0:T(8,128)S(1)} %param.35), channel_id=1, source_target_pairs={{0,1},{1,2},{2,3},{3,4},{4,5},{5,6},{6,7},{7,0},{8,9},{9,10},{10,1... | collective-permute-start | bytes 786440 | tf_op jit(solution)/shard_map/cond/branch_1_fun/ppermute | solution.py:19
  94.0 1.1 copy-start.7
  95.1 18.9 %collective-permute-start.8 = (f32[8,128,128]{2,1,0:T(8,128)S(1)}, f32[8,128,128]{2,1,0:T(8,128)S(1)}, u32[]{:S(2)}, u32[]{:S(2)}) collective-permute-start(f32[8,128,128]{2,1,0:T(8,128)S(1)} %param.22), channel_id=1, source_target_pairs={{0,6},{1,7},{2,0},{3,1},{4,2},{5,3},{6,4},{7,5},{8,14},{9,15},{10,... | collective-permute-start | bytes 1572872 | tf_op jit(solution)/shard_map/cond/branch_6_fun/ppermute | solution.py:19
  114.0 0.8 copy-start.4
  114.9 21.5 %copy-start.1 = (f32[32,64,384]{2,1,0:T(8,128)S(1)}, f32[32,64,384]{2,1,0:T(8,128)}, u32[]{:S(2)}) copy-start(f32[32,64,384]{2,1,0:T(8,128)} %all-gather.5.cloned.1.call-done) | copy-start | bytes 9437188
  114.9 17.6 %collective-permute-start.12 = (f32[6,128,128]{2,1,0:T(8,128)S(1)}, f32[6,128,128]{2,1,0:T(8,128)S(1)}, u32[]{:S(2)}, u32[]{:S(2)}) collective-permute-start(f32[6,128,128]{2,1,0:T(8,128)S(1)} %param.29), channel_id=1, source_target_pairs={{0,3},{1,4},{2,5},{3,6},{4,7},{5,0},{6,1},{7,2},{8,11},{9,12},{10,... | collective-permute-start | bytes 1179656 | tf_op jit(solution)/shard_map/cond/branch_3_fun/ppermute | solution.py:19
  132.7 2.5 copy-start.18
  132.7 3.1 copy-start.17
  139.7 5.2 %copy-start.15 = (pred[6]{0:T(512)(128)(4,1)S(1)}, pred[6]{0:T(512)(128)(4,1)}, u32[]{:S(2)}) copy-start(pred[6]{0:T(512)(128)(4,1)} %broadcast_compare_fusion.2) | copy-start | bytes 22
  141.7 4.9 %copy-start.8 = (f32[4,128,128]{2,1,0:T(8,128)S(1)}, f32[4,128,128]{2,1,0:T(8,128)}, u32[]{:S(2)}) copy-start(f32[4,128,128]{2,1,0:T(8,128)} %copy-done.7) | copy-start | bytes 786436
  144.9 3.1 copy-start.10
  145.5 3.9 %copy-start.5 = (f32[8,128,128]{2,1,0:T(8,128)S(1)}, f32[8,128,128]{2,1,0:T(8,128)}, u32[]{:S(2)}) copy-start(f32[8,128,128]{2,1,0:T(8,128)} %copy-done.4) | copy-start | bytes 1572868
  145.5 3.9 %copy-start.14 = (pred[8]{0:T(512)(128)(4,1)S(1)}, pred[8]{0:T(512)(128)(4,1)}, u32[]{:S(2)}) copy-start(pred[8]{0:T(512)(128)(4,1)} %broadcast_compare_fusion.3) | copy-start | bytes 28
  150.2 2.3 copy-start.3
  150.2 2.0 copy-start.2
  150.2 2.0 copy-start.12
  150.3 2.0 copy-start.13
  152.5 32.8 %collective-permute-start.40 = (f32[8,128,128]{2,1,0:T(8,128)S(1)}, f32[8,128,128]{2,1,0:T(8,128)S(1)}, u32[]{:S(2)}, u32[]{:S(2)}) collective-permute-start(f32[8,128,128]{2,1,0:T(8,128)S(1)} %dynamic-slice_bitcast_fusion), channel_id=1, source_target_pairs={{0,4},{1,5},{2,6},{3,7},{4,0},{5,1},{6,2},{7,3},{8,12},{9,13},{10,... | collective-permute-start | bytes 1572872 | tf_op jit(solution)/shard_map/ppermute | solution.py:187
  186.2 128.8 %all-reduce.6.cloned.1.call-start = ((), (), s32[]{:S(2)}) async-start(), calls=%async_computation.2 | async-start | bytes 4194304 | tf_op jit(solution)/shard_map/psum | solution.py:192
  264.3 1.2 copy-start.6
  264.3 1.7 copy-start.20
Sparse Core Ops, SparseCore 0:
  8.9 28.9 all-gather.4
  44.3 77.7 reduce-scatter.1
  186.4 73.2 all-gather.6
  264.4 50.5 all-reduce.5
